TPU v7x, 512 devices: a whole 4x4x16 slice. The times are simulated.
512 devices in a mesh: seq: 64 (over y, z), exp: 8 (over x, core).
Axes of the slice: x: 4, y: 4, z: 16, core: 2. Of those that a mesh axis runs over, the one named last changes fastest.
Arguments:
- tokens: bfloat16 [4096, 128], P('seq'), may hold values from -36 to 36
- norm_gains: float32 [2, 4096], P(None, 'seq'), may hold values from 0.1 to 1.9
- q_weight: bfloat16 [4096, 4096], P('seq', 'exp'), may hold values from -16 to 16
- kv_weight: bfloat16 [4096, 2, 1024], P('seq', None, 'exp'), may hold values from -1 to 1
- out_weight: bfloat16 [4096, 4096], P('seq', 'exp'), may hold values from -0.3 to 0.3
- kv_cache: bfloat16 [2, 512, 256, 1024], P(None, 'seq', None, 'exp'), may hold values from -8 to 8
- block_count: int32 [32], replicated, may hold values from 1 to 128, 512 in all
- placement: int32 [512], P('seq'), may hold values from 0 to 511, each once
- block_live: int32 [512], P('seq'), may hold values 0 or 1
- router_weight: bfloat16 [4096, 8], P('seq'), may hold values from -0.09375 to 0.09375
- routes: int32 [128, 2], replicated, may hold values from 0 to 7, all different within a row
- expert_in: bfloat16 [8, 2, 4096, 7168], P(None, None, 'seq', 'exp'), may hold values from -0.09375 to 0.09375
- expert_out: bfloat16 [8, 4096, 7168], P(None, 'seq', 'exp'), may hold values from -0.0625 to 0.0625
Outputs:
- layer_out: bfloat16 [4096, 128], P('seq')
Inputs may be any that keep to these rules, and one draw needn't show every extreme that they name: `block_count`: the counts sum to 512; the longest request holds exactly 128 blocks. `placement`: each pool slot holds a different block. `routes`: each row names two different experts.
All inputs are finite; a program needn't handle non-finite values. No bound on the sum of `block_live` on one device may be relied on, other than what follows from the above.
Results may differ from a plain program's by a relative error of at most 0.0065.
Values may be sent and summed in bfloat16 or wider, within the bound.
A program may use at most 128 MiB of HBM per device.

v0:
```python
import math
import jax
import jax.numpy as jnp
from jax import lax
from jax.sharding import PartitionSpec as P

D = 4096
HEAD_DIM = 128
TOPK = 2
NEGATIVE = -1e30
EPSILON = 1e-05


def block_owners(block_count, placement):
    starts = jnp.cumsum(block_count) - block_count
    before = (starts[None, :] <= placement[:, None]).astype(jnp.int32)
    return jnp.sum(before, axis=1) - 1


def softmax_join(first_part, second_part):
    joined_top = jnp.maximum(first_part[0], second_part[0])
    first_factor = jnp.exp(first_part[0] - joined_top)
    second_factor = jnp.exp(second_part[0] - joined_top)
    joined_total = first_part[1] * first_factor + second_part[1] * second_factor
    joined_sum = first_part[2] * first_factor[..., None] + second_part[2] * second_factor[..., None]
    return (joined_top, joined_total, joined_sum)


def per_device(
    tokens,
    norm_gains,
    q_weight,
    kv_weight,
    out_weight,
    kv_cache,
    block_count,
    placement,
    block_live,
    router_weight,
    routes,
    expert_in,
    expert_out,
):
    width_dev, row_total = tokens.shape
    requests = block_count.shape[0]
    steps_all = row_total // requests
    kv_heads_dev = kv_cache.shape[3] // HEAD_DIM
    heads_dev = q_weight.shape[1] // HEAD_DIM
    group_size = heads_dev // kv_heads_dev
    blocks_dev = kv_cache.shape[1]
    page_rows = kv_cache.shape[2]
    experts_all = expert_in.shape[0]
    ff_dev = expert_in.shape[3]
    score_scale = 1.0 / math.sqrt(HEAD_DIM)
    contract_first = (((0,), (0,)), ((), ()))
    token_float = tokens.astype(jnp.float32)
    normed = (token_float * norm_gains[0][:, None]).astype(jnp.bfloat16)
    query_part = lax.dot_general(
        normed, q_weight, contract_first, preferred_element_type=jnp.float32
    )
    fresh_part = lax.dot_general(
        normed, kv_weight.reshape(width_dev, -1), contract_first, preferred_element_type=jnp.float32
    )
    first_local = jnp.sum(token_float * token_float, axis=0)
    query_sum, fresh_sum, first_squares = lax.psum((query_part, fresh_part, first_local), "seq")
    attn_rms = lax.rsqrt(first_squares / D + EPSILON)
    queries = (
        (query_sum * attn_rms[:, None])
        .astype(jnp.bfloat16)
        .reshape(steps_all, requests, kv_heads_dev, group_size, HEAD_DIM)
    )
    fresh_rows = (
        (fresh_sum * attn_rms[:, None])
        .astype(jnp.bfloat16)
        .reshape(steps_all, requests, 2, kv_heads_dev, HEAD_DIM)
    )
    new_keys = fresh_rows[:, :, 0]
    new_values = fresh_rows[:, :, 1]
    cache_keys = kv_cache[0].reshape(blocks_dev, page_rows, kv_heads_dev, HEAD_DIM)
    cache_values = kv_cache[1].reshape(blocks_dev, page_rows, kv_heads_dev, HEAD_DIM)
    block_owner = block_owners(block_count, placement)
    block_alive = (block_live == 1)[:, None, None, None]
    member = (block_owner[:, None] == jnp.arange(requests)[None, :])[:, :, None, None, None]

    def attend(query_steps, first_step):
        step_count = query_steps.shape[0]
        picked = query_steps[:, block_owner]
        scores = (
            jnp.einsum("tpkgd,pjkd->pkgtj", picked, cache_keys, preferred_element_type=jnp.float32)
            * score_scale
        )
        block_top = jnp.max(scores, axis=-1)
        weights = jnp.exp(scores - block_top[..., None]).astype(jnp.bfloat16)
        block_total = jnp.sum(weights, axis=-1, dtype=jnp.float32)
        block_sum = jnp.einsum(
            "pkgtj,pjkd->pkgtd", weights, cache_values, preferred_element_type=jnp.float32
        )
        block_top = jnp.where(block_alive, block_top, NEGATIVE)
        block_total = jnp.where(block_alive, block_total, 0.0)
        block_sum = jnp.where(block_alive[..., None], block_sum, 0.0)
        local_top = jnp.max(jnp.where(member, block_top[:, None], NEGATIVE), axis=0)
        factor = jnp.where(
            member, jnp.exp(jnp.where(member, block_top[:, None] - local_top[None], NEGATIVE)), 0.0
        )
        local_total = jnp.sum(factor * block_total[:, None], axis=0)
        local_sum = jnp.einsum(
            "prkgt,pkgtd->rkgtd", factor, block_sum, precision=lax.Precision.HIGHEST
        )
        whole_top = lax.pmax(local_top, "seq")
        rescale = jnp.exp(local_top - whole_top)
        whole_total, whole_sum = lax.psum(
            (local_total * rescale, local_sum * rescale[..., None]), "seq"
        )
        new_scores = (
            jnp.einsum(
                "trkgd,srkd->rkgts", query_steps, new_keys, preferred_element_type=jnp.float32
            )
            * score_scale
        )
        causal = (first_step + jnp.arange(step_count))[:, None] >= jnp.arange(steps_all)[None, :]
        new_scores = jnp.where(causal, new_scores, NEGATIVE)
        new_top = jnp.max(new_scores, axis=-1)
        new_weights = jnp.where(causal, jnp.exp(new_scores - new_top[..., None]), 0.0).astype(
            jnp.bfloat16
        )
        new_total = jnp.sum(new_weights, axis=-1, dtype=jnp.float32)
        new_sum = jnp.einsum(
            "rkgts,srkd->rkgtd", new_weights, new_values, preferred_element_type=jnp.float32
        )
        joined_top, joined_total, joined_sum = softmax_join(
            (whole_top, whole_total, whole_sum), (new_top, new_total, new_sum)
        )
        attended = (joined_sum / joined_total[..., None]).astype(jnp.bfloat16)
        return jnp.transpose(attended, (3, 0, 1, 2, 4)).reshape(
            step_count * requests, heads_dev * HEAD_DIM
        )

    attention = jnp.concatenate(
        [
            attend(queries[step_index : step_index + 1], step_index)
            for step_index in range(steps_all)
        ],
        axis=0,
    )
    head_part = lax.dot_general(
        out_weight, attention, (((1,), (1,)), ((), ())), preferred_element_type=jnp.float32
    )
    residual = token_float + lax.psum(head_part, "exp")
    second_local = jnp.sum(residual * residual, axis=0)
    hidden_in = (residual * norm_gains[1][:, None]).astype(jnp.bfloat16)
    router_part = lax.dot_general(
        router_weight, hidden_in, contract_first, preferred_element_type=jnp.float32
    )
    expert_ids = jnp.arange(experts_all)
    chosen_part = jnp.sum(
        jnp.where(routes[:, :, None] == expert_ids[None, None, :], router_part.T[:, None, :], 0.0),
        axis=2,
    )
    flat_routes = routes.reshape(-1)
    pair_rows = row_total * TOPK
    second_squares, logit_sums = lax.psum((second_local, chosen_part), "seq")
    moe_rms = lax.rsqrt(second_squares / D + EPSILON)
    share_rows = pair_rows // lax.axis_size("seq")
    chosen = routes
    every_expert = lax.dot_general(
        hidden_in, expert_in, (((0,), (2,)), ((), ())), preferred_element_type=jnp.float32
    )
    one_hot = (chosen[:, :, None] == expert_ids[None, None, :]).astype(jnp.float32)
    result = jnp.einsum("ike,iecf->ikcf", one_hot, every_expert, precision=lax.Precision.HIGHEST)
    inputs = lax.psum_scatter(
        result.reshape(lax.axis_size("seq") * share_rows, 2 * ff_dev),
        "seq",
        scatter_dimension=0,
        tiled=True,
    )
    share_scale = lax.dynamic_slice_in_dim(
        jnp.repeat(moe_rms, TOPK), lax.axis_index("seq") * share_rows, share_rows, 0
    )
    inputs = inputs * share_scale[:, None]
    chosen = flat_routes
    product = lax.dot_general(
        expert_out,
        lax.all_gather(
            (jax.nn.silu(inputs[:, :ff_dev]) * inputs[:, ff_dev:]).astype(jnp.bfloat16),
            "seq",
            axis=0,
            tiled=True,
        ),
        (((2,), (1,)), ((), ())),
        preferred_element_type=jnp.float32,
    )
    picked = chosen[None, :] == expert_ids[:, None]
    expert_rows = jnp.sum(jnp.where(picked[:, None, :], product, 0.0), axis=0)
    logits = logit_sums * moe_rms[:, None]
    sigmoids = jax.nn.sigmoid(logits)
    gate_weights = sigmoids / jnp.sum(sigmoids, axis=1, keepdims=True)
    expert_part = jnp.sum(
        expert_rows.reshape(width_dev, row_total, TOPK) * gate_weights[None], axis=2
    )
    expert_total = lax.psum(expert_part.astype(jnp.bfloat16), "exp").astype(jnp.float32)
    return (residual + expert_total).astype(jnp.bfloat16)


def solution(mesh):
    return jax.shard_map(
        per_device,
        mesh=mesh,
        in_specs=(
            P("seq", None),
            P(None, "seq"),
            P("seq", "exp"),
            P("seq", None, "exp"),
            P("seq", "exp"),
            P(None, "seq", None, "exp"),
            P(),
            P("seq"),
            P("seq"),
            P("seq", None),
            P(),
            P(None, None, "seq", "exp"),
            P(None, "seq", "exp"),
        ),
        out_specs=P("seq", None),
        check_vma=False,
    )
```

profile of v0, /device:TPU:8, one launch (start us, length us, event | category | flops | bytes accessed | tf_op | source)
XLA Modules:
  0.0 1136.2 jit_solution(5942021511305152113)
XLA Ops:
  7.4 1.9 fusion.120
  12.5 128.0 %psum.106 = f32[128]{0:T(128)S(1)} all-reduce(f32[128]{0:T(128)S(1)} %fusion.58), channel_id=1, replica_groups=mesh['seq'=64,'exp'=8] {'seq'}, use_global_device_ids=true, to_apply=%region_2.0 | all-reduce | flops 128 | bytes 1024 | tf_op jit(solution)/shard_map/psum | solution.py:65
  142.0 1.7 fusion.59
  143.7 136.8 %all-reduce.9.cloned.1.call-done = f32[128,512]{1,0:T(8,128)} async-done(((f32[128,512]{1,0:T(8,128)}), f32[128,512]{1,0:T(8,128)}) %all-reduce.9.cloned.1.call-update) | async-done | bytes 262160 | tf_op jit(solution)/shard_map/psum | solution.py:65
  280.5 1.0 multiply_convert_fusion
  282.8 1.3 fusion.162
  288.7 122.6 %all-reduce.4 = (f32[32,1,4,1]{0,2,3,1:T(4,128)S(1)}, f32[32,1,4,1]{0,2,3,1:T(4,128)S(1)}, f32[32,1,4,1]{0,2,3,1:T(4,128)S(1)}, f32[32,1,4,1]{0,2,3,1:T(4,128)S(1)}) all-reduce(f32[32,1,4,1]{0,2,3,1:T(4,128)S(1)} %bitcast.383, f32[32,1,4,1]{0,2,3,1:T(4,128)S(1)} %bitcast.389, ...), channel_id=1, replica_groups=mesh['seq'=64,'exp'=8] {'seq'}, use_global_device_ids=true, to_apply=%region_35.36 | all-reduce | flops 512 | bytes 4096 | tf_op jit(solution)/shard_map/pmax | solution.py:109
  411.3 1.0 fusion.5
  412.3 1.0 fusion.7
  413.4 1.0 fusion.9
  414.4 1.0 fusion.11
  415.5 136.6 %all-reduce.2 = (f32[32,1,4,1]{0,2,3,1:T(4,128)S(1)}, f32[32,1,4,1]{0,2,3,1:T(4,128)S(1)}, f32[32,1,4,1]{0,2,3,1:T(4,128)S(1)}, f32[32,1,4,1]{0,2,3,1:T(4,128)S(1)}) all-reduce(f32[32,1,4,1]{0,2,3,1:T(4,128)S(1)} %get-tuple-element.62, f32[32,1,4,1]{0,2,3,1:T(4,128)S(1)} %get-tuple-element.60, ...), channel_id=1, replica_groups=mesh['seq'=64,'exp'=8] {'seq'}, use_global_device_ids=true, to_apply=%region_40.41 | all-reduce | flops 512 | bytes 4096 | tf_op jit(solution)/shard_map/psum | solution.py:111
  552.1 139.3 %all-reduce.13.cloned.1.call-done = (f32[128,256]{1,0:T(8,128)}, f32[32,1,4,1,128]{4,0,2,3,1:T(8,128)}, f32[32,1,4,1,128]{4,0,2,3,1:T(8,128)}, f32[32,1,4,1,128]{4,0,2,3,1:T(8,128)}, f32[32,1,4,1,128]{4,0,2,3,1:T(8,128)}) async-done(((f32[128,256]{1,0:T(8,128)}, f32[32,1,4,1,128]{4,0,2,3,1:T(8,128)}, f32[32,1,4,1,128]{4,0,2,3,1:T(8,128)}, f32[32,1,4,1,128]{4,0,2,3,1:T(8,128)}, ...) | async-done | bytes 393232 | tf_op jit(solution)/shard_map/psum | solution.py:65
  691.4 1.0 multiply_convert_fusion.1
  697.3 23.6 %psum.116 = f32[64,128]{1,0:T(8,128)S(1)} all-reduce(f32[64,128]{1,0:T(8,128)S(1)} %convolution_bitcast_fusion.5), channel_id=1, replica_groups=mesh['seq'=64,'exp'=8] {'exp'}, use_global_device_ids=true, to_apply=%region_42.43 | all-reduce | flops 8192 | bytes 65536 | tf_op jit(solution)/shard_map/psum | solution.py:148
  721.0 1.1 fusion.70
  722.1 6.5 fusion
  729.6 1.3 copy.269
  731.2 1.3 dynamic-slice
  733.7 120.3 %all-reduce.1 = (f32[128]{0:T(128)S(1)}, f32[128,2]{0,1:T(2,128)S(1)}) all-reduce(f32[128]{0:T(128)S(1)} %get-tuple-element.42, f32[128,2]{0,1:T(2,128)S(1)} %copy.252), channel_id=1, replica_groups=mesh['seq'=64,'exp'=8] {'seq'}, use_global_device_ids=true, to_apply=%region_45.46 | all-reduce | flops 384 | bytes 3072 | tf_op jit(solution)/shard_map/psum | solution.py:161
  854.5 149.4 %all-reduce.11.cloned.1.call-done = f32[256,1792]{1,0:T(8,128)} async-done(((f32[256,1792]{1,0:T(8,128)}), f32[256,1792]{1,0:T(8,128)}) %all-reduce.11.cloned.1.call-update) | async-done | bytes 1835024
  1004.8 98.4 %all-gather = bf16[64,4,896]{2,1,0:T(4,128)(2,1)S(1)} all-gather(bf16[1,4,896]{2,1,0:T(4,128)(2,1)S(1)} %fusion.118), channel_id=1, replica_groups=mesh['seq'=64,'exp'=8] {'seq'}, dimensions={0}, use_global_device_ids=true | all-gather | bytes 465920 | tf_op jit(solution)/shard_map/all_gather | solution.py:183
  1103.3 1.7 fusion.3
  1105.4 23.6 %psum.119 = bf16[64,128]{1,0:T(8,128)(2,1)S(1)} all-reduce(bf16[64,128]{1,0:T(8,128)(2,1)S(1)} %copy.254), channel_id=1, replica_groups=mesh['seq'=64,'exp'=8] {'exp'}, use_global_device_ids=true, to_apply=%region_51.52 | all-reduce | flops 8192 | bytes 32768 | tf_op jit(solution)/shard_map/psum | solution.py:200
  (136 shorter events, 20.4 us)
Async XLA Ops:
  6.5 714.4 %copy-start = (bf16[8,2,64,896]{3,2,1,0:T(8,128)(2,1)S(1)}, bf16[8,2,64,896]{3,2,1,0:T(8,128)(2,1)}, u32[]{:S(2)}) copy-start(bf16[8,2,64,896]{3,2,1,0:T(8,128)(2,1)} %param.24) | copy-start | bytes 5505028
  6.5 277.6 %copy-start.1 = (bf16[2,8,256,128]{3,2,1,0:T(8,128)(2,1)S(1)}, bf16[2,8,256,128]{3,2,1,0:T(8,128)(2,1)}, u32[]{:S(2)}) copy-start(bf16[2,8,256,128]{3,2,1,0:T(8,128)(2,1)} %param.18) | copy-start | bytes 3145732
  6.5 274.0 %all-reduce.9.cloned.1.call-start = ((), (), s32[]{:S(2)}) async-start(), calls=%async_computation | async-start | bytes 524288 | tf_op jit(solution)/shard_map/psum | solution.py:65
  9.3 682.1 %all-reduce.13.cloned.1.call-start = ((), (), s32[]{:S(2)}) async-start(), calls=%async_computation.2 | async-start | bytes 786432 | tf_op jit(solution)/shard_map/psum | solution.py:65
  415.4 588.5 %all-reduce.11.cloned.1.call-start = ((), (), s32[]{:S(2)}) async-start(), calls=%async_computation.1 | async-start | bytes 3670016
  691.4 3.7 copy-start.5
  691.4 4.6 copy-start.4
  692.5 4.5 copy-start.3
  692.6 4.5 copy-start.7
  693.1 27.8 %copy-start.2 = (bf16[64,128]{1,0:T(8,128)(2,1)S(1)}, bf16[64,128]{1,0:T(8,128)(2,1)}, u32[]{:S(2)}) copy-start(bf16[64,128]{1,0:T(8,128)(2,1)} %param.13) | copy-start | bytes 49156
  731.0 2.1 copy-start.6
Sparse Core Ops, SparseCore 0:
  10.8 269.7 all-reduce.8
  415.5 275.8 all-reduce.12
  731.1 272.7 all-reduce.10
where the time goes:
time: 1140 us
  blocking collectives  653 us (57%)
  waiting for transfers between devices  426 us (37%)
  matrix products  22.1 us (2%)
  between operations  14.3 us (1%)
    psum x2, waiting for transfers between devices, per_device(): lax.psum((query_part, fresh_part, first_local), 'seq')  276 us
    unnamed x4, waiting for transfers between devices  149 us
    psum x1, blocking collectives, attend(): lax.psum((local_total * rescale, local_sum * rescale[..., None]), 'seq')  137 us
    psum x1, blocking collectives, per_device(): lax.psum((query_part, fresh_part, first_local), 'seq')  128 us
    pmax x1, blocking collectives, attend(): whole_top = lax.pmax(local_top, 'seq')  123 us
    psum x1, blocking collectives, per_device(): second_squares, logit_sums = lax.psum((second_local, chosen_part), 'seq')  120 us
    all_gather x1, blocking collectives, per_device(): lax.all_gather((jax.nn.silu(inputs[:, :ff_dev]) * inputs[:, ff_dev:]).ast...  98.4 us
    psum x1, blocking collectives, per_device(): residual = token_float + lax.psum(head_part, 'exp')  23.6 us
  transfers between devices with their start and end apart: 3, of which 3 were waited for; matrix products, arithmetic and copies ran while one was open for 1% of the time, Pallas kernels for 0%

commit v1 on v0

--- a/solution.py
+++ b/solution.py
@@ -178,14 +178,12 @@
     )
     inputs = inputs * share_scale[:, None]
     chosen = flat_routes
+    settle_wall = lambda x_part: jnp.concatenate(
+        lax.all_to_all(jnp.stack([x_part] * lax.axis_size("seq"), 0), "seq", 0, 0), 0
+    )
     product = lax.dot_general(
         expert_out,
-        lax.all_gather(
-            (jax.nn.silu(inputs[:, :ff_dev]) * inputs[:, ff_dev:]).astype(jnp.bfloat16),
-            "seq",
-            axis=0,
-            tiled=True,
-        ),
+        settle_wall((jax.nn.silu(inputs[:, :ff_dev]) * inputs[:, ff_dev:]).astype(jnp.bfloat16)),
         (((2,), (1,)), ((), ())),
         preferred_element_type=jnp.float32,
     )

time: 1140 us -> 1070 us (0.939)
  blocking collectives: 653 us -> 555 us
  waiting for transfers between devices: 426 us -> 446 us
    all_gather x1 -> x0, blocking collectives: 98.4 us -> none  [per_device(): lax.all_gather((jax.nn.silu(inputs[:, :ff_dev]) * inputs[:, ff_dev:]).ast...]
    all_to_all x0 -> x1, waiting for transfers between devices: none -> 20.4 us  [per_device(): lax.all_to_all(jnp.stack([x_part] * lax.axis_size('seq'), 0), 'seq', 0, 0)]
  transfers between devices with their start and end apart: 3 -> 4, of which waited for: 3 -> 4; matrix products, arithmetic and copies ran while one was open for 1% -> 1% of each run, Pallas kernels for 0% -> 0%
where the time goes in v1:
time: 1070 us
  blocking collectives  555 us (52%)
  waiting for transfers between devices  446 us (42%)
  matrix products  22.1 us (2%)
  between operations  14.3 us (1%)
  local copies, waits for them, and re-layouts  11.8 us (1%)
    psum x2, waiting for transfers between devices, per_device(): lax.psum((query_part, fresh_part, first_local), 'seq')  276 us
    unnamed x4, waiting for transfers between devices  150 us
    psum x1, blocking collectives, attend(): lax.psum((local_total * rescale, local_sum * rescale[..., None]), 'seq')  137 us
    psum x1, blocking collectives, per_device(): lax.psum((query_part, fresh_part, first_local), 'seq')  128 us
    pmax x1, blocking collectives, attend(): whole_top = lax.pmax(local_top, 'seq')  123 us
    psum x1, blocking collectives, per_device(): second_squares, logit_sums = lax.psum((second_local, chosen_part), 'seq')  120 us
    psum x1, blocking collectives, per_device(): residual = token_float + lax.psum(head_part, 'exp')  23.6 us
    psum x1, blocking collectives, per_device(): lax.psum(expert_part.astype(jnp.bfloat16), 'exp').astype(jnp.float32)  23.6 us
  transfers between devices with their start and end apart: 4, of which 4 were waited for; matrix products, arithmetic and copies ran while one was open for 1% of the time, Pallas kernels for 0%

profile of v1, /device:TPU:8, one launch (start us, length us, event | category | flops | bytes accessed | tf_op | source)
XLA Modules:
  0.0 1069.5 jit_solution(13972998597743066660)
XLA Ops:
  7.4 1.9 fusion.119
  12.5 128.0 %psum.106 = f32[128]{0:T(128)S(1)} all-reduce(f32[128]{0:T(128)S(1)} %fusion.58), channel_id=1, replica_groups=mesh['seq'=64,'exp'=8] {'seq'}, use_global_device_ids=true, to_apply=%region_2.0 | all-reduce | flops 128 | bytes 1024 | tf_op jit(solution)/shard_map/psum | solution.py:65
  142.0 1.7 fusion.59
  143.7 136.8 %all-reduce.9.cloned.1.call-done = f32[128,512]{1,0:T(8,128)} async-done(((f32[128,512]{1,0:T(8,128)}), f32[128,512]{1,0:T(8,128)}) %all-reduce.9.cloned.1.call-update) | async-done | bytes 262160 | tf_op jit(solution)/shard_map/psum | solution.py:65
  280.5 1.0 multiply_convert_fusion
  282.8 1.3 fusion.161
  288.7 122.6 %all-reduce.4 = (f32[32,1,4,1]{0,2,3,1:T(4,128)S(1)}, f32[32,1,4,1]{0,2,3,1:T(4,128)S(1)}, f32[32,1,4,1]{0,2,3,1:T(4,128)S(1)}, f32[32,1,4,1]{0,2,3,1:T(4,128)S(1)}) all-reduce(f32[32,1,4,1]{0,2,3,1:T(4,128)S(1)} %bitcast.381, f32[32,1,4,1]{0,2,3,1:T(4,128)S(1)} %bitcast.387, ...), channel_id=1, replica_groups=mesh['seq'=64,'exp'=8] {'seq'}, use_global_device_ids=true, to_apply=%region_35.36 | all-reduce | flops 512 | bytes 4096 | tf_op jit(solution)/shard_map/pmax | solution.py:109
  411.3 1.0 fusion.5
  412.3 1.0 fusion.7
  413.4 1.0 fusion.9
  415.5 136.6 %all-reduce.2 = (f32[32,1,4,1]{0,2,3,1:T(4,128)S(1)}, f32[32,1,4,1]{0,2,3,1:T(4,128)S(1)}, f32[32,1,4,1]{0,2,3,1:T(4,128)S(1)}, f32[32,1,4,1]{0,2,3,1:T(4,128)S(1)}) all-reduce(f32[32,1,4,1]{0,2,3,1:T(4,128)S(1)} %get-tuple-element.62, f32[32,1,4,1]{0,2,3,1:T(4,128)S(1)} %get-tuple-element.60, ...), channel_id=1, replica_groups=mesh['seq'=64,'exp'=8] {'seq'}, use_global_device_ids=true, to_apply=%region_40.41 | all-reduce | flops 512 | bytes 4096 | tf_op jit(solution)/shard_map/psum | solution.py:111
  552.1 139.3 %all-reduce.13.cloned.1.call-done = (f32[128,256]{1,0:T(8,128)}, f32[32,1,4,1,128]{4,0,2,3,1:T(8,128)}, f32[32,1,4,1,128]{4,0,2,3,1:T(8,128)}, f32[32,1,4,1,128]{4,0,2,3,1:T(8,128)}, f32[32,1,4,1,128]{4,0,2,3,1:T(8,128)}) async-done(((f32[128,256]{1,0:T(8,128)}, f32[32,1,4,1,128]{4,0,2,3,1:T(8,128)}, f32[32,1,4,1,128]{4,0,2,3,1:T(8,128)}, f32[32,1,4,1,128]{4,0,2,3,1:T(8,128)}, ...) | async-done | bytes 393232 | tf_op jit(solution)/shard_map/psum | solution.py:65
  691.4 1.0 multiply_convert_fusion.1
  697.3 23.6 %psum.116 = f32[64,128]{1,0:T(8,128)S(1)} all-reduce(f32[64,128]{1,0:T(8,128)S(1)} %convolution_bitcast_fusion.5), channel_id=1, replica_groups=mesh['seq'=64,'exp'=8] {'exp'}, use_global_device_ids=true, to_apply=%region_42.43 | all-reduce | flops 8192 | bytes 65536 | tf_op jit(solution)/shard_map/psum | solution.py:148
  721.0 1.1 fusion.70
  722.1 6.5 fusion
  729.6 1.3 copy.269
  731.0 1.3 dynamic-slice
  733.5 120.3 %all-reduce.1 = (f32[128]{0:T(128)S(1)}, f32[128,2]{0,1:T(2,128)S(1)}) all-reduce(f32[128]{0:T(128)S(1)} %get-tuple-element.42, f32[128,2]{0,1:T(2,128)S(1)} %copy.252), channel_id=1, replica_groups=mesh['seq'=64,'exp'=8] {'seq'}, use_global_device_ids=true, to_apply=%region_45.46 | all-reduce | flops 384 | bytes 3072 | tf_op jit(solution)/shard_map/psum | solution.py:161
  854.2 149.5 %all-reduce.11.cloned.1.call-done = f32[256,1792]{1,0:T(8,128)} async-done(((f32[256,1792]{1,0:T(8,128)}), f32[256,1792]{1,0:T(8,128)}) %all-reduce.11.cloned.1.call-update) | async-done | bytes 1835024
  1005.6 10.3 all-to-all-start
  1016.1 20.4 %all-to-all-done = bf16[64,4,896]{2,1,0:T(4,128)(2,1)S(1)} async-done(((bf16[64,4,896]{2,1,0:T(4,128)(2,1)}), bf16[64,4,896]{2,1,0:T(4,128)(2,1)S(1)}, u32[]{:S(2)}, u32[]{:S(2)}) %all-to-all-start) | async-done | bytes 458784 | tf_op jit(solution)/shard_map/all_to_all | solution.py:182
  1036.6 1.7 fusion.3
  1038.7 23.6 %psum.119 = bf16[64,128]{1,0:T(8,128)(2,1)S(1)} all-reduce(bf16[64,128]{1,0:T(8,128)(2,1)S(1)} %copy.254), channel_id=1, replica_groups=mesh['seq'=64,'exp'=8] {'exp'}, use_global_device_ids=true, to_apply=%region_51.52 | all-reduce | flops 8192 | bytes 32768 | tf_op jit(solution)/shard_map/psum | solution.py:198
  (138 shorter events, 22.3 us)
Async XLA Ops:
  6.5 714.4 %copy-start = (bf16[8,2,64,896]{3,2,1,0:T(8,128)(2,1)S(1)}, bf16[8,2,64,896]{3,2,1,0:T(8,128)(2,1)}, u32[]{:S(2)}) copy-start(bf16[8,2,64,896]{3,2,1,0:T(8,128)(2,1)} %param.24) | copy-start | bytes 5505028
  6.5 277.6 %copy-start.1 = (bf16[2,8,256,128]{3,2,1,0:T(8,128)(2,1)S(1)}, bf16[2,8,256,128]{3,2,1,0:T(8,128)(2,1)}, u32[]{:S(2)}) copy-start(bf16[2,8,256,128]{3,2,1,0:T(8,128)(2,1)} %param.18) | copy-start | bytes 3145732
  6.5 274.0 %all-reduce.9.cloned.1.call-start = ((), (), s32[]{:S(2)}) async-start(), calls=%async_computation.1 | async-start | bytes 524288 | tf_op jit(solution)/shard_map/psum | solution.py:65
  9.3 682.1 %all-reduce.13.cloned.1.call-start = ((), (), s32[]{:S(2)}) async-start(), calls=%async_computation.3 | async-start | bytes 786432 | tf_op jit(solution)/shard_map/psum | solution.py:65
  415.4 588.4 %all-reduce.11.cloned.1.call-start = ((), (), s32[]{:S(2)}) async-start(), calls=%async_computation.2 | async-start | bytes 3670016
  691.4 3.7 copy-start.5
  691.4 4.6 copy-start.4
  692.5 4.5 copy-start.3
  692.6 4.5 copy-start.7
  693.1 27.8 %copy-start.2 = (bf16[64,128]{1,0:T(8,128)(2,1)S(1)}, bf16[64,128]{1,0:T(8,128)(2,1)}, u32[]{:S(2)}) copy-start(bf16[64,128]{1,0:T(8,128)(2,1)} %param.13) | copy-start | bytes 49156
  731.0 2.0 copy-start.6
  1005.6 30.9 %all-to-all-start = ((bf16[64,4,896]{2,1,0:T(4,128)(2,1)}), bf16[64,4,896]{2,1,0:T(4,128)(2,1)S(1)}, u32[]{:S(2)}, u32[]{:S(2)}) async-start(bf16[64,4,896]{2,1,0:T(4,128)(2,1)} %stack.2), calls=%async_computation | async-start | bytes 917504 | tf_op jit(solution)/shard_map/all_to_all | solution.py:182
Sparse Core Ops, SparseCore 0:
  10.8 269.7 all-reduce.8
  415.5 275.8 all-reduce.12
  731.1 272.5 all-reduce.10
